TPU v7x, 32 devices: a whole 2x2x4 slice. The times are simulated.
32 devices in a mesh: group: 2 (over y), slab: 4 (over z), subj: 2 (over x), yslab: 2 (over core).
Axes of the slice: x: 2, y: 2, z: 4, core: 2. Of those that a mesh axis runs over, the one named last changes fastest.
Arguments:
- subjects: bfloat16 [4, 64, 16, 256], P(('group', 'subj'), 'slab', 'yslab'), parts along dimension 0, may hold values from -6 to 6
- offsets: int32 [4, 3, 64, 16, 256], P(('group', 'subj'), None, 'slab', 'yslab'), parts along dimension 0, may hold values from -2 to 1
- template: float32 [128, 16, 256], P(('group', 'slab'), 'yslab'), parts along dimension 0, may hold values from -6 to 6
- control: float32 [4, 3, 19, 7, 128], P(('group', 'subj')), parts along dimension 0, may hold values from -8 to 8
Outputs:
- template_out: float32 [128, 16, 256], P(('group', 'slab'), 'yslab'), parts along dimension 0
- control_out: float32 [4, 3, 19, 7, 128], P(('group', 'subj')), parts along dimension 0
There are 2 independent parts, one for each index of `group`. A program takes and returns all parts, laid end to end along the dimension named above; each array names one. Nothing has to cross between parts.
All inputs are finite; a program needn't handle non-finite values.
Results may differ from a plain program's by a relative error of at most 0.00065.
Values may be sent and summed in bfloat16 or wider, within the bound.
A program may use at most 64 MiB of HBM per device.

v0:
```python
import jax
import jax.numpy as jnp
from jax import lax
from jax.sharding import PartitionSpec as P

KNOT = 4
KNOT_X = 2
HALO = 2
ITERS = 2
step_length = 0.5
tiny_term = 1e-06


def extended_2(value, sides, width):
    for axis, dim in sides:
        peers, length = (lax.axis_size(axis), value.shape[dim])
        up = [(i, (i + 1) % peers) for i in range(peers - 1)]
        down = [(j, i) for i, j in up]
        last = lax.slice_in_dim(value, length - width, length, axis=dim)
        initial = lax.slice_in_dim(value, 0, width, axis=dim)
        before = lax.ppermute(last, axis, up)
        after = lax.ppermute(initial, axis, down)
        value = jnp.concatenate([before, value, after], axis=dim)
    return value


def shifted(block, axis, distance):
    devices = range(lax.axis_size(axis))
    route = [(i - distance, i) for i in devices if i - distance in devices]
    return lax.ppermute(block, axis, route)


def from_root(value, axis, source):
    kept = jnp.where(lax.axis_index(axis) == source, value, 0).astype(value.dtype)
    return lax.psum(kept, axis)


def basis(positions, columns, spacing, wrap):
    cell = positions // spacing
    frac = (positions - cell * spacing).astype(jnp.float32) / spacing
    weights = [
        (1.0 - frac) ** 3 / 6.0,
        (3.0 * frac**3 - 6.0 * frac**2 + 4.0) / 6.0,
        (-3.0 * frac**3 + 3.0 * frac**2 + 3.0 * frac + 1.0) / 6.0,
        frac**3 / 6.0,
    ]
    index = jnp.arange(columns, dtype=jnp.int32)
    matrix = jnp.zeros((positions.shape[0], columns), jnp.float32)
    for offset in range(4):
        target = cell + offset
        if wrap:
            target = target % columns
        matrix = matrix + jnp.where(
            index[None, :] == target[:, None], weights[offset][:, None], 0.0
        )
    return matrix


def forward_field(coeffs, basis_z, basis_y, basis_x):
    high = lax.Precision.HIGHEST
    first = jnp.einsum("cabg,za->czbg", coeffs, basis_z, precision=high)
    second = jnp.einsum("czbg,yb->czyg", first, basis_y, precision=high)
    return jnp.einsum("czyg,xg->czyx", second, basis_x, precision=high)


def adjoint_field(gradient, basis_z, basis_y, basis_x):
    high = lax.Precision.HIGHEST
    first = jnp.einsum("czyx,xg->czyg", gradient, basis_x, precision=high)
    second = jnp.einsum("czyg,yb->czbg", first, basis_y, precision=high)
    return jnp.einsum("czbg,za->cabg", second, basis_z, precision=high)


def choose(shift_of, table, lead):
    result = table[-HALO + lead]
    for value in range(-HALO + 1, HALO):
        result = jnp.where(shift_of == value, table[value + lead], result)
    return result


def trilinear_local(volume, shifts, fraction, depth, height, width):
    frac_z, frac_y, frac_x = (fraction[0], fraction[1], fraction[2])
    shift_z, shift_y, shift_x = (shifts[0], shifts[1], shifts[2])
    along_y_of = {}
    diff_y_of = {}
    diff_xy_of = {}
    for move_z in range(-HALO, HALO + 1):
        along_x_of = {}
        diff_x_of = {}
        for move_y in range(-HALO, HALO + 1):
            plane = volume[
                move_z + HALO : move_z + HALO + depth, move_y + HALO : move_y + HALO + height, :
            ].astype(jnp.float32)
            columns = {}
            for move_x in range(-HALO, HALO + 1):
                columns[move_x] = plane[:, :, move_x + HALO : move_x + HALO + width]
            low = choose(shift_x, columns, 0)
            high = choose(shift_x, columns, 1)
            along_x_of[move_y] = low * (1.0 - frac_x) + high * frac_x
            diff_x_of[move_y] = high - low
        along_low = choose(shift_y, along_x_of, 0)
        along_high = choose(shift_y, along_x_of, 1)
        diff_low = choose(shift_y, diff_x_of, 0)
        diff_high = choose(shift_y, diff_x_of, 1)
        along_y_of[move_z] = along_low * (1.0 - frac_y) + along_high * frac_y
        diff_y_of[move_z] = along_high - along_low
        diff_xy_of[move_z] = diff_low * (1.0 - frac_y) + diff_high * frac_y
    along_y = [choose(shift_z, along_y_of, 0), choose(shift_z, along_y_of, 1)]
    diff_y = [choose(shift_z, diff_y_of, 0), choose(shift_z, diff_y_of, 1)]
    diff_xy = [choose(shift_z, diff_xy_of, 0), choose(shift_z, diff_xy_of, 1)]
    warped = along_y[0] * (1.0 - frac_z) + along_y[1] * frac_z
    slope_z = along_y[1] - along_y[0]
    slope_y = diff_y[0] * (1.0 - frac_z) + diff_y[1] * frac_z
    slope_x = diff_xy[0] * (1.0 - frac_z) + diff_xy[1] * frac_z
    return (warped, jnp.stack([slope_z, slope_y, slope_x]))


def shards(subjects, offsets, template, control):
    local_subjects = subjects.shape[0]
    depth, height, width = (subjects.shape[1], subjects.shape[2], subjects.shape[3])
    rows_slab = depth // KNOT
    cohort = local_subjects * lax.axis_size("subj")
    extended = extended_2(subjects, (("slab", 1), ("yslab", 2)), HALO)
    extended = jnp.pad(extended, ((0, 0), (0, 0), (0, 0), (HALO, HALO)))
    basis_z = basis(jnp.arange(depth, dtype=jnp.int32), rows_slab + 3, KNOT, False)
    y_start = lax.axis_index("yslab") * height
    basis_y = basis(y_start + jnp.arange(height, dtype=jnp.int32), control.shape[3], KNOT, False)
    basis_x = basis(jnp.arange(width, dtype=jnp.int32), control.shape[4], KNOT_X, True)
    first_row = lax.axis_index("slab") * rows_slab
    current = template
    coeffs_all = control
    for iteration in range(ITERS):
        band_coeffs = lax.dynamic_slice_in_dim(coeffs_all[0], first_row, rows_slab + 3, 1)
        displace = forward_field(band_coeffs, basis_z, basis_y, basis_x)
        tanh_u = jnp.tanh(displace)
        fraction = 0.5 + 0.5 * tanh_u
        warped, slopes = trilinear_local(extended[0], offsets[0], fraction, depth, height, width)
        resid = warped - current
        grad_u = resid[None] * slopes * (1.0 - tanh_u * tanh_u)
        band_list = [adjoint_field(grad_u, basis_z, basis_y, basis_x)]
        band_grid = jnp.stack(band_list)
        current = lax.psum(warped, "subj") / cohort
        band_grid = lax.psum(band_grid.astype(jnp.bfloat16), "yslab").astype(jnp.float32)
        head_rows = band_grid[:, :, :rows_slab]
        tail_part = band_grid[:, :, rows_slab:]
        carried = shifted(tail_part, "slab", 1)
        head_rows = head_rows.at[:, :, :3].add(carried)
        owned = lax.all_gather(head_rows.astype(jnp.bfloat16), "slab", axis=2, tiled=True).astype(
            head_rows.dtype
        )
        last_part = from_root(tail_part, "slab", lax.axis_size("slab") - 1)
        grid = jnp.concatenate([owned, last_part], axis=2)
        lengths = jnp.sqrt(jnp.sum(grid * grid, axis=1))
        peak = jnp.max(lengths, axis=(1, 2, 3))
        coeffs_all = coeffs_all - step_length * grid / (peak[:, None, None, None, None] + tiny_term)
    return (current, coeffs_all)


def solution(mesh):
    in_specs = (
        P(("group", "subj"), "slab", "yslab", None),
        P(("group", "subj"), None, "slab", "yslab", None),
        P(("group", "slab"), "yslab", None),
        P(("group", "subj"), None, None, None, None),
    )
    out_specs = (P(("group", "slab"), "yslab", None), P(("group", "subj"), None, None, None, None))
    return jax.shard_map(shards, mesh=mesh, in_specs=in_specs, out_specs=out_specs, check_vma=False)
```

profile of v0, /device:TPU:0, one launch (start us, length us, event | category | flops | bytes accessed | tf_op | source)
XLA Modules:
  0.0 160.3 jit_solution(13082636263804256856)
XLA Ops:
  7.2 0.7 fusion.363
  7.9 1.3 collective-permute-start.1
  9.2 5.6 %collective-permute-start = (bf16[1,2,8,256]{3,2,1,0:T(8,128)(2,1)S(1)}, bf16[1,2,8,256]{3,2,1,0:T(8,128)(2,1)S(1)}, u32[]{:S(2)}, u32[]{:S(2)}) collective-permute-start(bf16[1,2,8,256]{3,2,1,0:T(8,128)(2,1)S(1)} %get-tuple-element.162), channel_id=1, source_target_pairs={{0,4},{4,8},{8,12},{1,5},{5,9},{9,13},{2,6},{6,10},{10,14},{3,7},{... | collective-permute-start | bytes 24584 | tf_op jit(solution)/shard_map/ppermute | solution.py:21
  15.2 0.9 constant_dynamic-slice_fusion
  16.2 0.4 convolution_bitcast_fusion.3
  16.7 0.4 convolution_bitcast_fusion.1
  17.1 0.4 copy-done.65
  17.6 1.5 collective-permute-start.2
  19.0 1.3 collective-permute-start.3
  20.4 1.5 multiply_add_fusion.1
  22.8 0.6 copy-done.59
  23.7 0.3 fusion.38
  24.2 0.3 fusion.46
  24.6 0.3 fusion.44
  24.9 0.6 copy-done.64
  25.5 3.3 %fusion.335 = (f32[16,8,256]{2,1,0:T(8,128)S(1)}, f32[16,8,256]{2,1,0:T(8,128)}, f32[16,8,256]{2,1,0:T(8,128)S(1)}, f32[16,8,256]{2,1,0:T(8,128)S(1)}, f32[16,8,...) fusion(f32[16,8,256]{2,1,0:T(8,128)S(1)} %copy-done.64, ...), kind=kLoop, calls=%fused_computation.598 | loop fusion | flops 8093696 | bytes 21266432 | tf_op jit(solution)/shard_map/sub | solution.py:137
  30.5 2.9 %add_bitcast_fusion.2 = (f32[1,16,8,256]{3,2,1,0:T(8,128)S(1)}, f32[16,8,256]{2,1,0:T(8,128)}, f32[16,8,256]{2,1,0:T(8,128)}, f32[16,8,256]{2,1,0:T(8,128)}, f32...) fusion(pred[1,1,16,8,256]{4,3,2,1,0:T(8,128)(4,1)S(1)} %get-tup, ...), kind=kLoop, calls=%fused_computation.248 | loop fusion | flops 2654208 | bytes 8454144 | tf_op jit(solution)/shard_map/stack | solution.py:114
  33.4 0.6 copy-done.70
  34.1 0.8 fusion.4
  35.1 0.4 fusion.217
  35.9 4.2 %psum.42 = bf16[1,3,7,7,128]{4,2,3,1,0:T(8,128)(2,1)S(1)} all-reduce(bf16[1,3,7,7,128]{4,2,3,1,0:T(8,128)(2,1)S(1)} %fusion), channel_id=1, replica_groups=mesh['group'=2,'slab'=4,'subj'=2,'yslab'=2] {'yslab'}, use_global_device_ids=true, to_apply=%region_0.1 | all-reduce | flops 18816 | bytes 75264 | tf_op jit(solution)/shard_map/psum | solution.py:142
  40.2 0.6 copy-done.45
  40.8 3.8 %collective-permute-start.4 = (f32[1,3,3,7,128]{4,2,3,1,0:T(4,128)S(1)}, f32[1,3,3,7,128]{4,2,3,1,0:T(4,128)S(1)}, u32[]{:S(2)}, u32[]{:S(2)}) collective-permute-start(f32[1,3,3,7,128]{4,2,3,1,0:T(4,128)S(1)} %slice.1053), channel_id=1, source_target_pairs={{0,4},{4,8},{8,12},{1,5},{5,9},{9,13},{2,6},{6,10},{10,14},{3,7},{... | collective-permute-start | bytes 96776 | tf_op jit(solution)/shard_map/ppermute | solution.py:30
  44.6 17.6 %psum.43 = f32[1,3,3,7,128]{4,2,3,1,0:T(4,128)S(1)} all-reduce(f32[1,3,3,7,128]{4,2,3,1,0:T(4,128)S(1)} %broadcast_select_fusion.1), channel_id=1, replica_groups=mesh['group'=2,'slab'=4,'subj'=2,'yslab'=2] {'slab'}, use_global_device_ids=true, to_apply=%region_1.2 | all-reduce | flops 8064 | bytes 64512 | tf_op jit(solution)/shard_map/psum | solution.py:35
  62.3 0.7 slice-done
  63.2 13.4 %all_gather.6 = bf16[1,3,16,7,128]{4,3,1,0,2:T(8,128)(2,1)S(1)} all-gather(bf16[1,3,4,7,128]{4,3,1,0,2:T(8,128)(2,1)S(1)} %copy.8), channel_id=1, replica_groups=mesh['group'=2,'slab'=4,'subj'=2,'yslab'=2] {'slab'}, dimensions={2}, use_global_device_ids=true | all-gather | bytes 107520 | tf_op jit(solution)/shard_map/all_gather | solution.py:147
  76.6 0.7 fusion.174
  78.1 1.1 copy_subtract_fusion
  79.2 0.4 convolution_bitcast_fusion.2
  79.7 0.4 convolution_bitcast_fusion
  80.2 1.5 multiply_add_fusion
  81.9 3.0 %subtract_bitcast_fusion = (f32[1,16,8,256]{3,2,1,0:T(8,128)}, f32[16,8,256]{2,1,0:T(8,128)S(1)}, f32[16,8,256]{2,1,0:T(8,128)S(1)}, f32[16,8,256]{2,1,0:T(8,128...) fusion(pred[1,1,16,8,256]{4,3,2,1,0:T(8,128)(4,1)S(1)} %get-tup, ...), kind=kLoop, calls=%fused_computation.191 | loop fusion | flops 4227072 | bytes 8716288 | tf_op jit(solution)/shard_map/stack | solution.py:114
  84.9 0.8 add_bitcast_fusion.1
  86.2 0.5 copy-done.47
  87.0 20.5 %all-reduce.4.cloned.1.call-done = (f32[16,8,256]{2,1,0:T(8,128)}, f32[16,8,256]{2,1,0:T(8,128)}) async-done(((f32[16,8,256]{2,1,0:T(8,128)}, f32[16,8,256]{2,1,0:T(8,128)}), (f32[16,8,256]{2,1,0:T(8,128)}, f32[16,8,256]{2,1,0:T(8,128)})) %all-reduce.4.cloned.1.call-update) | async-done | bytes 262160 | tf_op jit(solution)/shard_map/psum | solution.py:141
  107.5 0.9 multiply_subtract_fusion
  108.5 0.6 copy-done.68
  109.1 0.8 fusion.11
  110.1 0.4 fusion.214
  111.0 3.5 %psum.46 = bf16[1,3,7,7,128]{4,2,3,1,0:T(8,128)(2,1)S(1)} all-reduce(bf16[1,3,7,7,128]{4,2,3,1,0:T(8,128)(2,1)S(1)} %fusion.1), channel_id=1, replica_groups=mesh['group'=2,'slab'=4,'subj'=2,'yslab'=2] {'yslab'}, use_global_device_ids=true, to_apply=%region_6.7 | all-reduce | flops 18816 | bytes 75264 | tf_op jit(solution)/shard_map/psum | solution.py:142
  114.5 0.6 copy-done.46
  115.4 0.7 broadcast_multiply_fusion
  116.1 3.4 %collective-permute-start.5 = (f32[1,3,3,7,128]{4,2,3,1,0:T(4,128)S(1)}, f32[1,3,3,7,128]{4,2,3,1,0:T(4,128)S(1)}, u32[]{:S(2)}, u32[]{:S(2)}) collective-permute-start(f32[1,3,3,7,128]{4,2,3,1,0:T(4,128)S(1)} %slice.1059), channel_id=1, source_target_pairs={{0,4},{4,8},{8,12},{1,5},{5,9},{9,13},{2,6},{6,10},{10,14},{3,7},{... | collective-permute-start | bytes 96776 | tf_op jit(solution)/shard_map/ppermute | solution.py:30
  119.5 17.6 %psum.47 = f32[1,3,3,7,128]{4,2,3,1,0:T(4,128)S(1)} all-reduce(f32[1,3,3,7,128]{4,2,3,1,0:T(4,128)S(1)} %broadcast_select_fusion), channel_id=1, replica_groups=mesh['group'=2,'slab'=4,'subj'=2,'yslab'=2] {'slab'}, use_global_device_ids=true, to_apply=%region_7.8 | all-reduce | flops 8064 | bytes 64512 | tf_op jit(solution)/shard_map/psum | solution.py:35
  137.1 0.7 slice-done.1
  138.0 13.2 %all_gather.7 = bf16[1,3,16,7,128]{4,3,1,0,2:T(8,128)(2,1)S(1)} all-gather(bf16[1,3,4,7,128]{4,3,1,0,2:T(8,128)(2,1)S(1)} %copy.12), channel_id=1, replica_groups=mesh['group'=2,'slab'=4,'subj'=2,'yslab'=2] {'slab'}, dimensions={2}, use_global_device_ids=true | all-gather | bytes 107520 | tf_op jit(solution)/shard_map/all_gather | solution.py:147
  151.3 0.6 fusion.173
  152.6 0.9 copy.15
  (328 shorter events, 5.8 us)
Async XLA Ops:
  7.2 100.3 %all-reduce.4.cloned.1.call-start = ((), (), s32[]{:S(2)}) async-start(), calls=%async_computation | async-start | bytes 524288 | tf_op jit(solution)/shard_map/psum | solution.py:141
  7.9 9.6 %collective-permute-start.1 = (bf16[1,2,8,256]{3,2,1,0:T(8,128)(2,1)S(1)}, bf16[1,2,8,256]{3,2,1,0:T(8,128)(2,1)S(1)}, u32[]{:S(2)}, u32[]{:S(2)}) collective-permute-start(bf16[1,2,8,256]{3,2,1,0:T(8,128)(2,1)S(1)} %get-tuple-element.161), channel_id=1, source_target_pairs={{4,0},{8,4},{12,8},{5,1},{9,5},{13,9},{6,2},{10,6},{14,10},{7,3},{... | collective-permute-start | bytes 24584 | tf_op jit(solution)/shard_map/ppermute | solution.py:22
  9.2 7.9 %collective-permute-start = (bf16[1,2,8,256]{3,2,1,0:T(8,128)(2,1)S(1)}, bf16[1,2,8,256]{3,2,1,0:T(8,128)(2,1)S(1)}, u32[]{:S(2)}, u32[]{:S(2)}) collective-permute-start(bf16[1,2,8,256]{3,2,1,0:T(8,128)(2,1)S(1)} %get-tuple-element.162), channel_id=1, source_target_pairs={{0,4},{4,8},{8,12},{1,5},{5,9},{9,13},{2,6},{6,10},{10,14},{3,7},{... | collective-permute-start | bytes 24584 | tf_op jit(solution)/shard_map/ppermute | solution.py:21
  14.8 1.7 %copy-start.109 = (f32[8]{0:T(128)}, f32[8]{0:T(128)S(1)}, u32[]{:S(2)}) copy-start(f32[8]{0:T(128)S(1)} %get-tuple-element.178) | copy-start | bytes 100
  14.8 1.7 %copy-start.112 = (f32[8]{0:T(128)}, f32[8]{0:T(128)S(1)}, u32[]{:S(2)}) copy-start(f32[8]{0:T(128)S(1)} %get-tuple-element.179) | copy-start | bytes 100
  14.9 1.7 %copy-start.116 = (s32[8]{0:T(128)}, s32[8]{0:T(128)S(1)}, u32[]{:S(2)}) copy-start(s32[8]{0:T(128)S(1)} %get-tuple-element.182) | copy-start | bytes 100
  14.9 1.7 %copy-start.120 = (s32[8]{0:T(128)}, s32[8]{0:T(128)S(1)}, u32[]{:S(2)}) copy-start(s32[8]{0:T(128)S(1)} %get-tuple-element.183) | copy-start | bytes 100
  15.1 18.2 %copy-start.66 = (f32[256]{0:T(256)}, f32[256]{0:T(256)S(1)}, u32[]{:S(2)}) copy-start(f32[256]{0:T(256)S(1)} %get-tuple-element.189) | copy-start | bytes 3076
  15.2 5.2 %copy-start.69 = (s32[256]{0:T(256)}, s32[256]{0:T(256)S(1)}, u32[]{:S(2)}) copy-start(s32[256]{0:T(256)S(1)} %get-tuple-element.186) | copy-start | bytes 3076
  15.2 5.2 %copy-start.73 = (s32[256]{0:T(256)}, s32[256]{0:T(256)S(1)}, u32[]{:S(2)}) copy-start(s32[256]{0:T(256)S(1)} %get-tuple-element.187) | copy-start | bytes 3076
  17.1 3.3 %copy-start.77 = (s32[256]{0:T(256)}, s32[256]{0:T(256)S(1)}, u32[]{:S(2)}) copy-start(s32[256]{0:T(256)S(1)} %get-tuple-element.184) | copy-start | bytes 3076
  17.1 3.3 %copy-start.81 = (s32[256]{0:T(256)}, s32[256]{0:T(256)S(1)}, u32[]{:S(2)}) copy-start(s32[256]{0:T(256)S(1)} %get-tuple-element.185) | copy-start | bytes 3076
  17.6 4.3 %collective-permute-start.2 = (bf16[1,20,2,256]{3,2,1,0:T(2,128)(2,1)S(1)}, bf16[1,20,2,256]{3,2,1,0:T(2,128)(2,1)S(1)}, u32[]{:S(2)}, u32[]{:S(2)}) collective-permute-start(bf16[1,20,2,256]{3,2,1,0:T(2,128)(2,1)S(1)} %get-tuple-element.159), channel_id=1, source_target_pairs={{0,1},{2,3},{4,5},{6,7},{8,9},{10,11},{12,13},{14,15},{16,17},{18,... | collective-permute-start | bytes 61448 | tf_op jit(solution)/shard_map/ppermute | solution.py:21
  19.0 3.1 %collective-permute-start.3 = (bf16[1,20,2,256]{3,2,1,0:T(2,128)(2,1)S(1)}, bf16[1,20,2,256]{3,2,1,0:T(2,128)(2,1)S(1)}, u32[]{:S(2)}, u32[]{:S(2)}) collective-permute-start(bf16[1,20,2,256]{3,2,1,0:T(2,128)(2,1)S(1)} %get-tuple-element.160), channel_id=1, source_target_pairs={{1,0},{3,2},{5,4},{7,6},{9,8},{11,10},{13,12},{15,14},{17,16},{19,... | collective-permute-start | bytes 61448 | tf_op jit(solution)/shard_map/ppermute | solution.py:22
  30.5 2.9 %copy-start.57 = (f32[3,16,8,256]{3,2,1,0:T(8,128)S(1)}, f32[3,16,8,256]{3,2,1,0:T(8,128)}, u32[]{:S(2)}) copy-start(f32[3,16,8,256]{3,2,1,0:T(8,128)} %get-tuple-element.164) | copy-start | bytes 1179652
  30.5 2.9 %copy-start.74 = (s32[256]{0:T(256)S(1)}, s32[256]{0:T(256)}, u32[]{:S(2)}) copy-start(s32[256]{0:T(256)} %copy-done.73) | copy-start | bytes 3076
  30.5 2.9 %copy-start.78 = (s32[256]{0:T(256)S(1)}, s32[256]{0:T(256)}, u32[]{:S(2)}) copy-start(s32[256]{0:T(256)} %copy-done.77) | copy-start | bytes 3076
  30.5 2.9 %copy-start.82 = (s32[256]{0:T(256)S(1)}, s32[256]{0:T(256)}, u32[]{:S(2)}) copy-start(s32[256]{0:T(256)} %copy-done.81) | copy-start | bytes 3076
  40.8 21.4 %collective-permute-start.4 = (f32[1,3,3,7,128]{4,2,3,1,0:T(4,128)S(1)}, f32[1,3,3,7,128]{4,2,3,1,0:T(4,128)S(1)}, u32[]{:S(2)}, u32[]{:S(2)}) collective-permute-start(f32[1,3,3,7,128]{4,2,3,1,0:T(4,128)S(1)} %slice.1053), channel_id=1, source_target_pairs={{0,4},{4,8},{8,12},{1,5},{5,9},{9,13},{2,6},{6,10},{10,14},{3,7},{... | collective-permute-start | bytes 96776 | tf_op jit(solution)/shard_map/ppermute | solution.py:30
  78.0 2.1 %copy-start.71 = (s32[256]{0:T(256)S(1)}, s32[256]{0:T(256)}, u32[]{:S(2)}) copy-start(s32[256]{0:T(256)} %copy-done.69) | copy-start | bytes 3076
  78.0 2.1 %copy-start.75 = (s32[256]{0:T(256)S(1)}, s32[256]{0:T(256)}, u32[]{:S(2)}) copy-start(s32[256]{0:T(256)} %copy-done.73) | copy-start | bytes 3076
  78.0 2.1 %copy-start.79 = (s32[256]{0:T(256)S(1)}, s32[256]{0:T(256)}, u32[]{:S(2)}) copy-start(s32[256]{0:T(256)} %copy-done.77) | copy-start | bytes 3076
  78.0 2.1 %copy-start.83 = (s32[256]{0:T(256)S(1)}, s32[256]{0:T(256)}, u32[]{:S(2)}) copy-start(s32[256]{0:T(256)} %copy-done.81) | copy-start | bytes 3076
  78.0 3.7 %copy-start.30 = (f32[16,8,256]{2,1,0:T(8,128)S(1)}, f32[16,8,256]{2,1,0:T(8,128)}, u32[]{:S(2)}) copy-start(f32[16,8,256]{2,1,0:T(8,128)} %copy-done.29) | copy-start | bytes 393220
  78.0 3.7 %copy-start.32 = (f32[16,8,256]{2,1,0:T(8,128)S(1)}, f32[16,8,256]{2,1,0:T(8,128)}, u32[]{:S(2)}) copy-start(f32[16,8,256]{2,1,0:T(8,128)} %copy-done.31) | copy-start | bytes 393220
  78.1 3.7 %copy-start.34 = (f32[16,8,256]{2,1,0:T(8,128)S(1)}, f32[16,8,256]{2,1,0:T(8,128)}, u32[]{:S(2)}) copy-start(f32[16,8,256]{2,1,0:T(8,128)} %copy-done.33) | copy-start | bytes 393220
  78.1 3.7 %copy-start.36 = (f32[16,8,256]{2,1,0:T(8,128)S(1)}, f32[16,8,256]{2,1,0:T(8,128)}, u32[]{:S(2)}) copy-start(f32[16,8,256]{2,1,0:T(8,128)} %copy-done.35) | copy-start | bytes 393220
  78.1 3.7 %copy-start.38 = (f32[16,8,256]{2,1,0:T(8,128)S(1)}, f32[16,8,256]{2,1,0:T(8,128)}, u32[]{:S(2)}) copy-start(f32[16,8,256]{2,1,0:T(8,128)} %copy-done.37) | copy-start | bytes 393220
  79.1 2.6 %copy-start.28 = (f32[16,8,256]{2,1,0:T(8,128)S(1)}, f32[16,8,256]{2,1,0:T(8,128)}, u32[]{:S(2)}) copy-start(f32[16,8,256]{2,1,0:T(8,128)} %copy-done.27) | copy-start | bytes 393220
  79.2 2.6 %copy-start.24 = (f32[16,8,256]{2,1,0:T(8,128)S(1)}, f32[16,8,256]{2,1,0:T(8,128)}, u32[]{:S(2)}) copy-start(f32[16,8,256]{2,1,0:T(8,128)} %copy-done.23) | copy-start | bytes 393220
  79.2 2.6 %copy-start.26 = (f32[16,8,256]{2,1,0:T(8,128)S(1)}, f32[16,8,256]{2,1,0:T(8,128)}, u32[]{:S(2)}) copy-start(f32[16,8,256]{2,1,0:T(8,128)} %copy-done.25) | copy-start | bytes 393220
  79.7 2.2 %copy-start.16 = (f32[16,8,256]{2,1,0:T(8,128)S(1)}, f32[16,8,256]{2,1,0:T(8,128)}, u32[]{:S(2)}) copy-start(f32[16,8,256]{2,1,0:T(8,128)} %copy-done.15) | copy-start | bytes 393220
  79.7 2.2 %copy-start.18 = (f32[16,8,256]{2,1,0:T(8,128)S(1)}, f32[16,8,256]{2,1,0:T(8,128)}, u32[]{:S(2)}) copy-start(f32[16,8,256]{2,1,0:T(8,128)} %copy-done.17) | copy-start | bytes 393220
  79.7 2.2 %copy-start.20 = (f32[16,8,256]{2,1,0:T(8,128)S(1)}, f32[16,8,256]{2,1,0:T(8,128)}, u32[]{:S(2)}) copy-start(f32[16,8,256]{2,1,0:T(8,128)} %copy-done.19) | copy-start | bytes 393220
  79.7 2.2 %copy-start.22 = (f32[16,8,256]{2,1,0:T(8,128)S(1)}, f32[16,8,256]{2,1,0:T(8,128)}, u32[]{:S(2)}) copy-start(f32[16,8,256]{2,1,0:T(8,128)} %copy-done.21) | copy-start | bytes 393220
  80.1 1.7 %copy-start.2 = (f32[16,8,256]{2,1,0:T(8,128)S(1)}, f32[16,8,256]{2,1,0:T(8,128)}, u32[]{:S(2)}) copy-start(f32[16,8,256]{2,1,0:T(8,128)} %copy-done.1) | copy-start | bytes 393220
  80.2 1.7 %copy-start.4 = (f32[16,8,256]{2,1,0:T(8,128)S(1)}, f32[16,8,256]{2,1,0:T(8,128)}, u32[]{:S(2)}) copy-start(f32[16,8,256]{2,1,0:T(8,128)} %copy-done.3) | copy-start | bytes 393220
  80.2 1.7 %copy-start.6 = (f32[16,8,256]{2,1,0:T(8,128)S(1)}, f32[16,8,256]{2,1,0:T(8,128)}, u32[]{:S(2)}) copy-start(f32[16,8,256]{2,1,0:T(8,128)} %copy-done.5) | copy-start | bytes 393220
  80.2 1.7 %copy-start.8 = (f32[16,8,256]{2,1,0:T(8,128)S(1)}, f32[16,8,256]{2,1,0:T(8,128)}, u32[]{:S(2)}) copy-start(f32[16,8,256]{2,1,0:T(8,128)} %copy-done.7) | copy-start | bytes 393220
  80.2 1.7 %copy-start.10 = (f32[16,8,256]{2,1,0:T(8,128)S(1)}, f32[16,8,256]{2,1,0:T(8,128)}, u32[]{:S(2)}) copy-start(f32[16,8,256]{2,1,0:T(8,128)} %copy-done.9) | copy-start | bytes 393220
  86.8 20.7 %copy-start = (f32[16,8,256]{2,1,0:T(8,128)S(1)}, f32[16,8,256]{2,1,0:T(8,128)}, u32[]{:S(2)}) copy-start(f32[16,8,256]{2,1,0:T(8,128)} %get-tuple-element.116) | copy-start | bytes 393220
  86.8 21.6 %copy-start.62 = (f32[1,16,8,256]{3,2,1,0:T(8,128)S(1)}, f32[1,16,8,256]{3,2,1,0:T(8,128)}, u32[]{:S(2)}) copy-start(f32[1,16,8,256]{3,2,1,0:T(8,128)} %get-tuple-element.32) | copy-start | bytes 393220
  86.8 21.6 %copy-start.72 = (s32[256]{0:T(256)S(1)}, s32[256]{0:T(256)}, u32[]{:S(2)}) copy-start(s32[256]{0:T(256)} %copy-done.69) | copy-start | bytes 3076
  86.8 21.7 %copy-start.76 = (s32[256]{0:T(256)S(1)}, s32[256]{0:T(256)}, u32[]{:S(2)}) copy-start(s32[256]{0:T(256)} %copy-done.73) | copy-start | bytes 3076
  86.8 21.7 %copy-start.80 = (s32[256]{0:T(256)S(1)}, s32[256]{0:T(256)}, u32[]{:S(2)}) copy-start(s32[256]{0:T(256)} %copy-done.77) | copy-start | bytes 3076
  86.8 21.7 %copy-start.84 = (s32[256]{0:T(256)S(1)}, s32[256]{0:T(256)}, u32[]{:S(2)}) copy-start(s32[256]{0:T(256)} %copy-done.81) | copy-start | bytes 3076
  87.0 21.5 %copy-start.58 = (f32[3,16,8,256]{3,2,1,0:T(8,128)S(1)}, f32[3,16,8,256]{3,2,1,0:T(8,128)}, u32[]{:S(2)}) copy-start(f32[3,16,8,256]{3,2,1,0:T(8,128)} %get-tuple-element.167) | copy-start | bytes 1179652
  116.1 21.0 %collective-permute-start.5 = (f32[1,3,3,7,128]{4,2,3,1,0:T(4,128)S(1)}, f32[1,3,3,7,128]{4,2,3,1,0:T(4,128)S(1)}, u32[]{:S(2)}, u32[]{:S(2)}) collective-permute-start(f32[1,3,3,7,128]{4,2,3,1,0:T(4,128)S(1)} %slice.1059), channel_id=1, source_target_pairs={{0,4},{4,8},{8,12},{1,5},{5,9},{9,13},{2,6},{6,10},{10,14},{3,7},{... | collective-permute-start | bytes 96776 | tf_op jit(solution)/shard_map/ppermute | solution.py:30
  (101 other events, 104.9 us)
Sparse Core Ops, SparseCore 0:
  85.9 21.5 all-reduce.3
where the time goes:
time: 161 us; the launch traced here: 160 us
  blocking collectives  69.6 us (43%)
  waiting for transfers between devices  20.7 us (13%)
  between operations  17.3 us (11%)
  starting transfers between devices  16.8 us (10%)
  other arithmetic  16.6 us (10%)
  local copies, waits for them, and re-layouts  11.8 us (7%)
  matrix products  7.5 us (5%)
    psum x2, blocking collectives, from_root(): return lax.psum(kept, axis)  35.2 us
    all_gather x2, blocking collectives, shards(): lax.all_gather(head_rows.astype(jnp.bfloat16), 'slab', axis=2, tiled=True)  26.7 us
    psum x1, waiting for transfers between devices, shards(): current = lax.psum(warped, 'subj') / cohort  20.5 us
    unnamed x283, local copies, waits for them, and re-layouts  8.37 us
    psum x2, blocking collectives, shards(): lax.psum(band_grid.astype(jnp.bfloat16), 'yslab').astype(jnp.float32)  7.77 us
    ppermute x2, starting transfers between devices, shifted(): return lax.ppermute(block, axis, route)  7.15 us
    ppermute x2, starting transfers between devices, extended_2(): before = lax.ppermute(last, axis, up)  7.04 us
    another operation x6, other arithmetic, trilinear_local(): return (warped, jnp.stack([slope_z, slope_y, slope_x]))  6.89 us
  transfers between devices with their start and end apart: 7, of which 2 were waited for; matrix products, arithmetic and copies ran while one was open for 2% of the time, Pallas kernels for 0%

commit v1 on v0

--- a/solution.py
+++ b/solution.py
@@ -1,3 +1,4 @@
+import functools
 import jax
 import jax.numpy as jnp
 from jax import lax
@@ -9,6 +10,14 @@
 ITERS = 2
 step_length = 0.5
 tiny_term = 1e-06
+
+
+def finish_sector(message, which_axis):
+    q_next = lax.all_gather(message, which_axis).sum(axis=0)
+    return q_next
+
+
+open_pipes = functools.partial(finish_sector, which_axis="subj")
 
 
 def extended_2(value, sides, width):
@@ -138,7 +147,7 @@
         grad_u = resid[None] * slopes * (1.0 - tanh_u * tanh_u)
         band_list = [adjoint_field(grad_u, basis_z, basis_y, basis_x)]
         band_grid = jnp.stack(band_list)
-        current = lax.psum(warped, "subj") / cohort
+        current = open_pipes(warped) / cohort
         band_grid = lax.psum(band_grid.astype(jnp.bfloat16), "yslab").astype(jnp.float32)
         head_rows = band_grid[:, :, :rows_slab]
         tail_part = band_grid[:, :, rows_slab:]

time: 161 us -> 136 us (0.84)
  waiting for transfers between devices: 20.7 us -> 0.23 us
  between operations: 17.3 us -> 3.68 us
  blocking collectives: 69.6 us -> 82.2 us
  starting transfers between devices: 16.8 us -> 14.6 us
  matrix products: 7.5 us -> 9.57 us
  other arithmetic: 16.6 us -> 14.6 us
    psum x1 -> x0, waiting for transfers between devices: 20.5 us -> none  [shards(): current = lax.psum(warped, 'subj') / cohort]
    all_gather x0 -> x2, blocking collectives: none -> 12.6 us  [finish_sector(): q_next = lax.all_gather(message, which_axis).sum(axis=0)]
    another operation x6, other arithmetic: 6.89 us -> 2.13 us  [trilinear_local(): return (warped, jnp.stack([slope_z, slope_y, slope_x]))]
    ppermute x2, starting transfers between devices: 7.15 us -> 5.03 us  [shifted(): return lax.ppermute(block, axis, route)]
    unnamed x283 -> x219, local copies, waits for them, and re-layouts: 8.37 us -> 7.24 us
  transfers between devices with their start and end apart: 7 -> 6, of which waited for: 2 -> 1; matrix products, arithmetic and copies ran while one was open for 2% -> 5% of each run, Pallas kernels for 0% -> 0%
where the time goes in v1:
time: 136 us
  blocking collectives  82.2 us (60%)
  starting transfers between devices  14.6 us (11%)
  other arithmetic  14.6 us (11%)
  local copies, waits for them, and re-layouts  10.7 us (8%)
  matrix products  9.57 us (7%)
  between operations  3.68 us (3%)
    psum x2, blocking collectives, from_root(): return lax.psum(kept, axis)  35.1 us
    all_gather x2, blocking collectives, shards(): lax.all_gather(head_rows.astype(jnp.bfloat16), 'slab', axis=2, tiled=True)  26.7 us
    all_gather x2, blocking collectives, finish_sector(): q_next = lax.all_gather(message, which_axis).sum(axis=0)  12.6 us
    psum x2, blocking collectives, shards(): lax.psum(band_grid.astype(jnp.bfloat16), 'yslab').astype(jnp.float32)  7.75 us
    unnamed x219, local copies, waits for them, and re-layouts  7.24 us
    ppermute x2, starting transfers between devices, extended_2(): before = lax.ppermute(last, axis, up)  7.04 us
    sub x2, other arithmetic, shards(): resid = warped - current  5.17 us
    ppermute x2, starting transfers between devices, shifted(): return lax.ppermute(block, axis, route)  5.03 us
  transfers between devices with their start and end apart: 6, of which 1 were waited for; matrix products, arithmetic and copies ran while one was open for 5% of the time, Pallas kernels for 0%

profile of v1, /device:TPU:0, one launch (start us, length us, event | category | flops | bytes accessed | tf_op | source)
XLA Modules:
  0.0 135.6 jit_solution(2194223259681769177)
XLA Ops:
  0.6 0.7 fusion.363
  1.3 1.3 collective-permute-start.1
  2.6 5.6 %collective-permute-start = (bf16[1,2,8,256]{3,2,1,0:T(8,128)(2,1)S(1)}, bf16[1,2,8,256]{3,2,1,0:T(8,128)(2,1)S(1)}, u32[]{:S(2)}, u32[]{:S(2)}) collective-permute-start(bf16[1,2,8,256]{3,2,1,0:T(8,128)(2,1)S(1)} %get-tuple-element.159), channel_id=1, source_target_pairs={{0,4},{4,8},{8,12},{1,5},{5,9},{9,13},{2,6},{6,10},{10,14},{3,7},{... | collective-permute-start | bytes 24584 | tf_op jit(solution)/shard_map/ppermute | solution.py:30
  8.5 0.6 fusion.310
  9.1 0.6 and_select_fusion.5
  9.7 0.9 constant_dynamic-slice_fusion
  10.6 1.1 convolution_bitcast_fusion.3
  11.8 0.4 convolution_bitcast_fusion.1
  12.2 0.4 copy-done.65
  12.7 1.5 %collective-permute-start.2 = (bf16[1,20,2,256]{3,2,1,0:T(2,128)(2,1)S(1)}, bf16[1,20,2,256]{3,2,1,0:T(2,128)(2,1)S(1)}, u32[]{:S(2)}, u32[]{:S(2)}) collective-permute-start(bf16[1,20,2,256]{3,2,1,0:T(2,128)(2,1)S(1)} %get-tuple-element.156), channel_id=1, source_target_pairs={{0,1},{2,3},{4,5},{6,7},{8,9},{10,11},{12,13},{14,15},{16,17},{18,... | collective-permute-start | bytes 61448 | tf_op jit(solution)/shard_map/ppermute | solution.py:30
  14.2 1.3 collective-permute-start.3
  15.5 1.6 %multiply_add_fusion.1 = (f32[3,16,8,256]{3,2,1,0:T(8,128)S(1)}, f32[3,16,8,256]{3,2,1,0:T(8,128)}) fusion(f32[3,16,8,128]{3,2,1,0:T(8,128)S(1)} %convolution_bitcast_fusion.1, f32[256]{0:T(256)S(1)} %get-tuple-element.188, s32[256]{0:T(256)S(1)} %get-tuple-element.181, f32[256]{0:T(256)S(1)} %get-tuple-element.187, s32[256]{0:T(256)S(1)} %get-tuple-element.182, ...), kind=kOutput, calls=%fused_computation.32 | convolution fusion | flops 151552000 | bytes 991232 | tf_op jit(solution)/shard_map/czyg,xg->czyx/dot_general | solution.py:72
  17.9 0.7 copy-done.61
  20.0 0.6 copy-done.64
  20.6 2.6 %fusion.335 = (f32[16,8,256]{2,1,0:T(8,128)S(1)}, f32[16,8,256]{2,1,0:T(8,128)S(1)}, f32[16,8,256]{2,1,0:T(8,128)S(1)}, f32[16,8,256]{2,1,0:T(8,128)S(1)}, f32[1...) fusion(f32[16,8,256]{2,1,0:T(8,128)S(1)} %copy-done.64, ...), kind=kLoop, calls=%fused_computation.598 | loop fusion | flops 8093696 | bytes 21266432 | tf_op jit(solution)/shard_map/sub | solution.py:146
  25.2 1.7 %add_bitcast_fusion.2 = (f32[1,16,8,256]{3,2,1,0:T(8,128)S(1)}, f32[16,8,256]{2,1,0:T(8,128)}, f32[16,8,256]{2,1,0:T(8,128)}, f32[16,8,256]{2,1,0:T(8,128)}, f32...) fusion(pred[1,1,16,8,256]{4,3,2,1,0:T(8,128)(4,1)S(1)} %get-tup, ...), kind=kLoop, calls=%fused_computation.248 | loop fusion | flops 2654208 | bytes 8454144 | tf_op jit(solution)/shard_map/stack | solution.py:123
  27.0 0.8 fusion.4
  27.9 0.4 fusion.217
  28.4 0.9 fusion
  29.3 4.2 %psum.28 = bf16[1,3,7,7,128]{4,2,3,1,0:T(8,128)(2,1)S(1)} all-reduce(bf16[1,3,7,7,128]{4,2,3,1,0:T(8,128)(2,1)S(1)} %fusion), channel_id=1, replica_groups=mesh['group'=2,'slab'=4,'subj'=2,'yslab'=2] {'yslab'}, use_global_device_ids=true, to_apply=%region_0.1 | all-reduce | flops 18816 | bytes 75264 | tf_op jit(solution)/shard_map/psum | solution.py:151
  33.6 0.6 copy-done.48
  34.1 6.2 %all-gather.1 = f32[32,8,256]{2,1,0:T(8,128)S(1)} all-gather(f32[16,8,256]{2,1,0:T(8,128)S(1)} %get-tuple-element.45), channel_id=3, replica_groups=mesh['group'=2,'slab'=4,'subj'=2,'yslab'=2] {'subj'}, dimensions={0}, use_global_device_ids=true | all-gather | bytes 393216 | tf_op jit(solution)/shard_map/all_gather | solution.py:16
  40.4 3.7 %collective-permute-start.4 = (f32[1,3,3,7,128]{4,2,3,1,0:T(4,128)S(1)}, f32[1,3,3,7,128]{4,2,3,1,0:T(4,128)S(1)}, u32[]{:S(2)}, u32[]{:S(2)}) collective-permute-start(f32[1,3,3,7,128]{4,2,3,1,0:T(4,128)S(1)} %slice.1053), channel_id=1, source_target_pairs={{0,4},{4,8},{8,12},{1,5},{5,9},{9,13},{2,6},{6,10},{10,14},{3,7},{... | collective-permute-start | bytes 96776 | tf_op jit(solution)/shard_map/ppermute | solution.py:39
  44.2 17.6 %psum.29 = f32[1,3,3,7,128]{4,2,3,1,0:T(4,128)S(1)} all-reduce(f32[1,3,3,7,128]{4,2,3,1,0:T(4,128)S(1)} %broadcast_select_fusion.1), channel_id=1, replica_groups=mesh['group'=2,'slab'=4,'subj'=2,'yslab'=2] {'slab'}, use_global_device_ids=true, to_apply=%region_1.2 | all-reduce | flops 8064 | bytes 64512 | tf_op jit(solution)/shard_map/psum | solution.py:44
  61.8 0.7 reduce_sum.38
  62.5 0.7 slice-done
  63.4 13.4 %all_gather.18 = bf16[1,3,16,7,128]{4,3,1,0,2:T(8,128)(2,1)S(1)} all-gather(bf16[1,3,4,7,128]{4,3,1,0,2:T(8,128)(2,1)S(1)} %copy.8), channel_id=1, replica_groups=mesh['group'=2,'slab'=4,'subj'=2,'yslab'=2] {'slab'}, dimensions={2}, use_global_device_ids=true | all-gather | bytes 107520 | tf_op jit(solution)/shard_map/all_gather | solution.py:156
  76.9 0.7 fusion.174
  78.3 1.1 copy_subtract_fusion
  79.4 0.5 copy-done.77
  80.1 1.1 convolution_bitcast_fusion.2
  81.3 0.4 convolution_bitcast_fusion
  81.9 0.8 multiply_add_fusion
  83.0 2.5 %multiply_subtract_fusion = (f32[16,8,256]{2,1,0:T(8,128)S(1)}, f32[16,8,256]{2,1,0:T(8,128)S(1)}, f32[16,8,256]{2,1,0:T(8,128)S(1)}, f32[16,8,256]{2,1,0:T(8,12...) fusion(f32[16,8,256]{2,1,0:T(8,128)} %reduce_sum.38, ...), kind=kLoop, calls=%fused_computation.192 | loop fusion | flops 4390912 | bytes 9109504 | tf_op jit(solution)/shard_map/sub | solution.py:146
  85.7 0.8 copy-done.50
  86.9 0.8 fusion.11
  87.7 0.4 fusion.214
  88.1 0.9 fusion.1
  89.0 3.5 %psum.30 = bf16[1,3,7,7,128]{4,2,3,1,0:T(8,128)(2,1)S(1)} all-reduce(bf16[1,3,7,7,128]{4,2,3,1,0:T(8,128)(2,1)S(1)} %fusion.1), channel_id=1, replica_groups=mesh['group'=2,'slab'=4,'subj'=2,'yslab'=2] {'yslab'}, use_global_device_ids=true, to_apply=%region_6.7 | all-reduce | flops 18816 | bytes 75264 | tf_op jit(solution)/shard_map/psum | solution.py:151
  92.6 0.6 copy-done.49
  93.2 1.3 collective-permute-start.5
  94.5 6.4 %all-gather = f32[32,8,256]{2,1,0:T(8,128)S(1)} all-gather(f32[16,8,256]{2,1,0:T(8,128)S(1)} %get-tuple-element.31), channel_id=2, replica_groups=mesh['group'=2,'slab'=4,'subj'=2,'yslab'=2] {'subj'}, dimensions={0}, use_global_device_ids=true | all-gather | bytes 393216 | tf_op jit(solution)/shard_map/all_gather | solution.py:16
  100.9 0.7 broadcast_multiply_fusion
  101.6 17.5 %psum.31 = f32[1,3,3,7,128]{4,2,3,1,0:T(4,128)S(1)} all-reduce(f32[1,3,3,7,128]{4,2,3,1,0:T(4,128)S(1)} %broadcast_select_fusion), channel_id=1, replica_groups=mesh['group'=2,'slab'=4,'subj'=2,'yslab'=2] {'slab'}, use_global_device_ids=true, to_apply=%region_7.8 | all-reduce | flops 8064 | bytes 64512 | tf_op jit(solution)/shard_map/psum | solution.py:44
  119.2 0.7 slice-done.1
  120.0 13.3 %all_gather.23 = bf16[1,3,16,7,128]{4,3,1,0,2:T(8,128)(2,1)S(1)} all-gather(bf16[1,3,4,7,128]{4,3,1,0,2:T(8,128)(2,1)S(1)} %copy.12), channel_id=1, replica_groups=mesh['group'=2,'slab'=4,'subj'=2,'yslab'=2] {'slab'}, dimensions={2}, use_global_device_ids=true | all-gather | bytes 107520 | tf_op jit(solution)/shard_map/all_gather | solution.py:156
  133.4 0.6 fusion.173
  134.7 0.9 copy.15
  (265 shorter events, 5.7 us)
Async XLA Ops:
  1.3 11.3 %collective-permute-start.1 = (bf16[1,2,8,256]{3,2,1,0:T(8,128)(2,1)S(1)}, bf16[1,2,8,256]{3,2,1,0:T(8,128)(2,1)S(1)}, u32[]{:S(2)}, u32[]{:S(2)}) collective-permute-start(bf16[1,2,8,256]{3,2,1,0:T(8,128)(2,1)S(1)} %get-tuple-element.158), channel_id=1, source_target_pairs={{4,0},{8,4},{12,8},{5,1},{9,5},{13,9},{6,2},{10,6},{14,10},{7,3},{... | collective-permute-start | bytes 24584 | tf_op jit(solution)/shard_map/ppermute | solution.py:31
  2.6 9.6 %collective-permute-start = (bf16[1,2,8,256]{3,2,1,0:T(8,128)(2,1)S(1)}, bf16[1,2,8,256]{3,2,1,0:T(8,128)(2,1)S(1)}, u32[]{:S(2)}, u32[]{:S(2)}) collective-permute-start(bf16[1,2,8,256]{3,2,1,0:T(8,128)(2,1)S(1)} %get-tuple-element.159), channel_id=1, source_target_pairs={{0,4},{4,8},{8,12},{1,5},{5,9},{9,13},{2,6},{6,10},{10,14},{3,7},{... | collective-permute-start | bytes 24584 | tf_op jit(solution)/shard_map/ppermute | solution.py:30
  8.3 3.4 %copy-start.84 = (f32[8]{0:T(128)}, f32[8]{0:T(128)S(1)}, u32[]{:S(2)}) copy-start(f32[8]{0:T(128)S(1)} %get-tuple-element.175) | copy-start | bytes 100
  8.3 3.4 %copy-start.87 = (f32[8]{0:T(128)}, f32[8]{0:T(128)S(1)}, u32[]{:S(2)}) copy-start(f32[8]{0:T(128)S(1)} %get-tuple-element.176) | copy-start | bytes 100
  8.3 3.4 %copy-start.90 = (s32[8]{0:T(128)}, s32[8]{0:T(128)S(1)}, u32[]{:S(2)}) copy-start(s32[8]{0:T(128)S(1)} %get-tuple-element.179) | copy-start | bytes 100
  8.3 3.4 %copy-start.93 = (s32[8]{0:T(128)}, s32[8]{0:T(128)S(1)}, u32[]{:S(2)}) copy-start(s32[8]{0:T(128)S(1)} %get-tuple-element.180) | copy-start | bytes 100
  8.3 3.4 %copy-start.96 = (s32[8]{0:T(128)}, s32[8]{0:T(128)S(1)}, u32[]{:S(2)}) copy-start(s32[8]{0:T(128)S(1)} %get-tuple-element.167) | copy-start | bytes 100
  8.3 3.4 %copy-start.99 = (s32[8]{0:T(128)}, s32[8]{0:T(128)S(1)}, u32[]{:S(2)}) copy-start(s32[8]{0:T(128)S(1)} %get-tuple-element.168) | copy-start | bytes 100
  8.4 3.4 %copy-start.102 = (f32[8]{0:T(128)}, f32[8]{0:T(128)S(1)}, u32[]{:S(2)}) copy-start(f32[8]{0:T(128)S(1)} %get-tuple-element.169) | copy-start | bytes 100
  8.4 3.4 %copy-start.105 = (f32[8]{0:T(128)}, f32[8]{0:T(128)S(1)}, u32[]{:S(2)}) copy-start(f32[8]{0:T(128)S(1)} %get-tuple-element.170) | copy-start | bytes 100
  8.4 19.9 %copy-start.76 = (s32[16]{0:T(128)}, s32[16]{0:T(128)S(1)}, u32[]{:S(2)}) copy-start(s32[16]{0:T(128)S(1)} %get-tuple-element.177) | copy-start | bytes 196
  8.4 19.9 %copy-start.78 = (s32[16]{0:T(128)}, s32[16]{0:T(128)S(1)}, u32[]{:S(2)}) copy-start(s32[16]{0:T(128)S(1)} %get-tuple-element.178) | copy-start | bytes 196
  8.4 19.9 %copy-start.80 = (f32[16]{0:T(128)}, f32[16]{0:T(128)S(1)}, u32[]{:S(2)}) copy-start(f32[16]{0:T(128)S(1)} %get-tuple-element.173) | copy-start | bytes 196
  8.4 19.9 %copy-start.82 = (f32[16]{0:T(128)}, f32[16]{0:T(128)S(1)}, u32[]{:S(2)}) copy-start(f32[16]{0:T(128)S(1)} %get-tuple-element.174) | copy-start | bytes 196
  9.7 17.2 %copy-start.66 = (f32[256]{0:T(256)}, f32[256]{0:T(256)S(1)}, u32[]{:S(2)}) copy-start(f32[256]{0:T(256)S(1)} %get-tuple-element.186) | copy-start | bytes 3076
  9.7 17.2 %copy-start.68 = (s32[256]{0:T(256)}, s32[256]{0:T(256)S(1)}, u32[]{:S(2)}) copy-start(s32[256]{0:T(256)S(1)} %get-tuple-element.183) | copy-start | bytes 3076
  9.7 17.2 %copy-start.70 = (s32[256]{0:T(256)}, s32[256]{0:T(256)S(1)}, u32[]{:S(2)}) copy-start(s32[256]{0:T(256)S(1)} %get-tuple-element.184) | copy-start | bytes 3076
  12.2 14.7 %copy-start.72 = (s32[256]{0:T(256)}, s32[256]{0:T(256)S(1)}, u32[]{:S(2)}) copy-start(s32[256]{0:T(256)S(1)} %get-tuple-element.181) | copy-start | bytes 3076
  12.2 14.7 %copy-start.74 = (s32[256]{0:T(256)}, s32[256]{0:T(256)S(1)}, u32[]{:S(2)}) copy-start(s32[256]{0:T(256)S(1)} %get-tuple-element.182) | copy-start | bytes 3076
  12.7 4.3 %collective-permute-start.2 = (bf16[1,20,2,256]{3,2,1,0:T(2,128)(2,1)S(1)}, bf16[1,20,2,256]{3,2,1,0:T(2,128)(2,1)S(1)}, u32[]{:S(2)}, u32[]{:S(2)}) collective-permute-start(bf16[1,20,2,256]{3,2,1,0:T(2,128)(2,1)S(1)} %get-tuple-element.156), channel_id=1, source_target_pairs={{0,1},{2,3},{4,5},{6,7},{8,9},{10,11},{12,13},{14,15},{16,17},{18,... | collective-permute-start | bytes 61448 | tf_op jit(solution)/shard_map/ppermute | solution.py:30
  14.2 3.1 %collective-permute-start.3 = (bf16[1,20,2,256]{3,2,1,0:T(2,128)(2,1)S(1)}, bf16[1,20,2,256]{3,2,1,0:T(2,128)(2,1)S(1)}, u32[]{:S(2)}, u32[]{:S(2)}) collective-permute-start(bf16[1,20,2,256]{3,2,1,0:T(2,128)(2,1)S(1)} %get-tuple-element.157), channel_id=1, source_target_pairs={{1,0},{3,2},{5,4},{7,6},{9,8},{11,10},{13,12},{15,14},{17,16},{19,... | collective-permute-start | bytes 61448 | tf_op jit(solution)/shard_map/ppermute | solution.py:31
  25.2 1.8 %copy-start.60 = (f32[3,16,8,256]{3,2,1,0:T(8,128)S(1)}, f32[3,16,8,256]{3,2,1,0:T(8,128)}, u32[]{:S(2)}) copy-start(f32[3,16,8,256]{3,2,1,0:T(8,128)} %get-tuple-element.161) | copy-start | bytes 1179652
  40.4 22.1 %collective-permute-start.4 = (f32[1,3,3,7,128]{4,2,3,1,0:T(4,128)S(1)}, f32[1,3,3,7,128]{4,2,3,1,0:T(4,128)S(1)}, u32[]{:S(2)}, u32[]{:S(2)}) collective-permute-start(f32[1,3,3,7,128]{4,2,3,1,0:T(4,128)S(1)} %slice.1053), channel_id=1, source_target_pairs={{0,4},{4,8},{8,12},{1,5},{5,9},{9,13},{2,6},{6,10},{10,14},{3,7},{... | collective-permute-start | bytes 96776 | tf_op jit(solution)/shard_map/ppermute | solution.py:39
  78.2 3.1 %copy-start.86 = (f32[8]{0:T(128)S(1)}, f32[8]{0:T(128)}, u32[]{:S(2)}) copy-start(f32[8]{0:T(128)} %copy-done.84) | copy-start | bytes 100
  78.2 3.1 %copy-start.89 = (f32[8]{0:T(128)S(1)}, f32[8]{0:T(128)}, u32[]{:S(2)}) copy-start(f32[8]{0:T(128)} %copy-done.87) | copy-start | bytes 100
  78.2 3.1 %copy-start.92 = (s32[8]{0:T(128)S(1)}, s32[8]{0:T(128)}, u32[]{:S(2)}) copy-start(s32[8]{0:T(128)} %copy-done.90) | copy-start | bytes 100
  78.2 3.1 %copy-start.95 = (s32[8]{0:T(128)S(1)}, s32[8]{0:T(128)}, u32[]{:S(2)}) copy-start(s32[8]{0:T(128)} %copy-done.93) | copy-start | bytes 100
  78.2 3.1 %copy-start.98 = (s32[8]{0:T(128)S(1)}, s32[8]{0:T(128)}, u32[]{:S(2)}) copy-start(s32[8]{0:T(128)} %copy-done.96) | copy-start | bytes 100
  78.2 3.1 %copy-start.101 = (s32[8]{0:T(128)S(1)}, s32[8]{0:T(128)}, u32[]{:S(2)}) copy-start(s32[8]{0:T(128)} %copy-done.99) | copy-start | bytes 100
  78.2 3.1 %copy-start.104 = (f32[8]{0:T(128)S(1)}, f32[8]{0:T(128)}, u32[]{:S(2)}) copy-start(f32[8]{0:T(128)} %copy-done.102) | copy-start | bytes 100
  78.2 3.1 %copy-start.107 = (f32[8]{0:T(128)S(1)}, f32[8]{0:T(128)}, u32[]{:S(2)}) copy-start(f32[8]{0:T(128)} %copy-done.105) | copy-start | bytes 100
  78.3 4.4 %copy-start.29 = (f32[16,8,256]{2,1,0:T(8,128)S(1)}, f32[16,8,256]{2,1,0:T(8,128)}, u32[]{:S(2)}) copy-start(f32[16,8,256]{2,1,0:T(8,128)} %copy-done.28) | copy-start | bytes 393220
  78.3 4.4 %copy-start.31 = (f32[16,8,256]{2,1,0:T(8,128)S(1)}, f32[16,8,256]{2,1,0:T(8,128)}, u32[]{:S(2)}) copy-start(f32[16,8,256]{2,1,0:T(8,128)} %copy-done.30) | copy-start | bytes 393220
  78.3 4.4 %copy-start.33 = (f32[16,8,256]{2,1,0:T(8,128)S(1)}, f32[16,8,256]{2,1,0:T(8,128)}, u32[]{:S(2)}) copy-start(f32[16,8,256]{2,1,0:T(8,128)} %copy-done.32) | copy-start | bytes 393220
  78.3 4.4 %copy-start.35 = (f32[16,8,256]{2,1,0:T(8,128)S(1)}, f32[16,8,256]{2,1,0:T(8,128)}, u32[]{:S(2)}) copy-start(f32[16,8,256]{2,1,0:T(8,128)} %copy-done.34) | copy-start | bytes 393220
  78.3 4.4 %copy-start.37 = (f32[16,8,256]{2,1,0:T(8,128)S(1)}, f32[16,8,256]{2,1,0:T(8,128)}, u32[]{:S(2)}) copy-start(f32[16,8,256]{2,1,0:T(8,128)} %copy-done.36) | copy-start | bytes 393220
  79.4 3.3 %copy-start.27 = (f32[16,8,256]{2,1,0:T(8,128)S(1)}, f32[16,8,256]{2,1,0:T(8,128)}, u32[]{:S(2)}) copy-start(f32[16,8,256]{2,1,0:T(8,128)} %copy-done.26) | copy-start | bytes 393220
  80.1 1.7 %copy-start.75 = (s32[256]{0:T(256)S(1)}, s32[256]{0:T(256)}, u32[]{:S(2)}) copy-start(s32[256]{0:T(256)} %copy-done.74) | copy-start | bytes 3076
  80.1 2.6 %copy-start.23 = (f32[16,8,256]{2,1,0:T(8,128)S(1)}, f32[16,8,256]{2,1,0:T(8,128)}, u32[]{:S(2)}) copy-start(f32[16,8,256]{2,1,0:T(8,128)} %copy-done.22) | copy-start | bytes 393220
  80.1 2.6 %copy-start.25 = (f32[16,8,256]{2,1,0:T(8,128)S(1)}, f32[16,8,256]{2,1,0:T(8,128)}, u32[]{:S(2)}) copy-start(f32[16,8,256]{2,1,0:T(8,128)} %copy-done.24) | copy-start | bytes 393220
  83.0 2.6 %copy-start.53 = (f32[16,8,256]{2,1,0:T(8,128)S(1)}, f32[16,8,256]{2,1,0:T(8,128)}, u32[]{:S(2)}) copy-start(f32[16,8,256]{2,1,0:T(8,128)} %get-tuple-element.103) | copy-start | bytes 393220
  83.0 2.6 %copy-start.54 = (f32[16,8,256]{2,1,0:T(8,128)S(1)}, f32[16,8,256]{2,1,0:T(8,128)}, u32[]{:S(2)}) copy-start(f32[16,8,256]{2,1,0:T(8,128)} %get-tuple-element.104) | copy-start | bytes 393220
  83.0 2.7 %copy-start.55 = (f32[16,8,256]{2,1,0:T(8,128)S(1)}, f32[16,8,256]{2,1,0:T(8,128)}, u32[]{:S(2)}) copy-start(f32[16,8,256]{2,1,0:T(8,128)} %get-tuple-element.105) | copy-start | bytes 393220
  83.0 2.7 %copy-start.56 = (f32[16,8,256]{2,1,0:T(8,128)S(1)}, f32[16,8,256]{2,1,0:T(8,128)}, u32[]{:S(2)}) copy-start(f32[16,8,256]{2,1,0:T(8,128)} %get-tuple-element.106) | copy-start | bytes 393220
  83.0 2.7 %copy-start.57 = (f32[16,8,256]{2,1,0:T(8,128)S(1)}, f32[16,8,256]{2,1,0:T(8,128)}, u32[]{:S(2)}) copy-start(f32[16,8,256]{2,1,0:T(8,128)} %get-tuple-element.107) | copy-start | bytes 393220
  83.0 2.7 %copy-start.58 = (f32[16,8,256]{2,1,0:T(8,128)S(1)}, f32[16,8,256]{2,1,0:T(8,128)}, u32[]{:S(2)}) copy-start(f32[16,8,256]{2,1,0:T(8,128)} %get-tuple-element.108) | copy-start | bytes 393220
  83.0 2.7 %copy-start.59 = (f32[16,8,256]{2,1,0:T(8,128)S(1)}, f32[16,8,256]{2,1,0:T(8,128)}, u32[]{:S(2)}) copy-start(f32[16,8,256]{2,1,0:T(8,128)} %get-tuple-element.109) | copy-start | bytes 393220
  93.2 25.9 %collective-permute-start.5 = (f32[1,3,3,7,128]{4,2,3,1,0:T(4,128)S(1)}, f32[1,3,3,7,128]{4,2,3,1,0:T(4,128)S(1)}, u32[]{:S(2)}, u32[]{:S(2)}) collective-permute-start(f32[1,3,3,7,128]{4,2,3,1,0:T(4,128)S(1)} %slice.1059), channel_id=1, source_target_pairs={{0,4},{4,8},{8,12},{1,5},{5,9},{9,13},{2,6},{6,10},{10,14},{3,7},{... | collective-permute-start | bytes 96776 | tf_op jit(solution)/shard_map/ppermute | solution.py:39
  (68 other events, 73.8 us)
